TPU v7x, 256 devices: a whole 4x4x8 slice. The times are simulated.
256 devices in a mesh: freq: 64 (over y, z, core), sky: 4 (over x).
Axes of the slice: x: 4, y: 4, z: 8, core: 2. Of those that a mesh axis runs over, the one named last changes fastest.
Arguments:
- sky_maps: bfloat16 [1024, 96, 4096], P('freq', 'sky'), may hold values from -240 to 240
- beam_index: int32 [1024], P('freq'), may hold values from 0 to 7
- beam_taps: float32 [8, 31], replicated, may hold values from 0.05 to 1
- start_seed: int32 [1024, 16], replicated, may hold values from -64 to 64
Outputs:
- cleaned: bfloat16 [1024, 256, 1536], P(None, ('freq', 'sky'))
All inputs are finite; a program needn't handle non-finite values.
Results may differ from a plain program's by a relative error of at most 0.0079.
The roundings to bfloat16 on the way count: a program that leaves them out, or rounds other values in their place, can miss the bound.
Values may be sent and summed in bfloat16 or wider, within the bound.
No kernel may reach another device: no remote copies, remote signals or barrier semaphores. Data moves between devices by JAX's collectives and lax.ppermute only.
A program may use at most 64 MiB of HBM per device.

v0:
```python
import jax
import jax.numpy as jnp
from jax import lax
from jax.sharding import PartitionSpec as P

ITERS = 8


def with_halo(x, sides, width):
    for axis, dim in sides:
        size, length = (lax.axis_size(axis), x.shape[dim])
        up = [(i, (i + 1) % size) for i in range(size - 1)]
        down = [(j, i) for i, j in up]
        last = lax.slice_in_dim(x, length - width, length, axis=dim)
        leading = lax.slice_in_dim(x, 0, width, axis=dim)
        before = lax.ppermute(last, axis, up)
        after = lax.ppermute(leading, axis, down)
        x = jnp.concatenate([before, x, after], axis=dim)
    return x


def column_pass(padded, kernels, strip_rows, half_taps, tap_count):
    row_pass = jnp.zeros((padded.shape[0], strip_rows, padded.shape[2]), jnp.float32)
    for offset in range(tap_count):
        row_pass = row_pass + kernels[:, offset, None, None] * padded[
            :, offset : offset + strip_rows, :
        ].astype(jnp.float32)
    columns = padded.shape[2]
    widened = jnp.pad(row_pass, ((0, 0), (0, 0), (half_taps, half_taps)))
    col_pass = jnp.zeros(row_pass.shape, jnp.float32)
    for offset in range(tap_count):
        col_pass = (
            col_pass + kernels[:, offset, None, None] * widened[:, :, offset : offset + columns]
        )
    return col_pass.astype(jnp.bfloat16)


def orthonormal(images):
    gram_matrix = jnp.dot(images.T, images, precision=lax.Precision.HIGHEST)
    factor = jnp.linalg.cholesky(gram_matrix)
    return lax.linalg.triangular_solve(
        factor, images, left_side=False, lower=True, transpose_a=True
    )


def local_covariance(tile_data):
    return lax.dot_general(
        tile_data, tile_data, (((1,), (1,)), ((), ())), preferred_element_type=jnp.float32
    )


def body(sky_maps, beam_index, beam_taps, start_seed):
    channels, strip_rows, columns = sky_maps.shape
    beam_count, tap_count = beam_taps.shape
    half_taps = (tap_count - 1) // 2
    onehot = (beam_index[:, None] == jnp.arange(beam_count, dtype=jnp.int32)[None, :]).astype(
        jnp.float32
    )
    tap_rows = jnp.dot(onehot, beam_taps, precision=lax.Precision.HIGHEST)
    kernels = tap_rows / jnp.sum(tap_rows, axis=1, keepdims=True)
    padded = with_halo(sky_maps, (("sky", 1),), half_taps)
    smoothed = column_pass(padded, kernels, strip_rows, half_taps, tap_count)
    freq_count = lax.axis_size("freq")
    sky_count = lax.axis_size("sky")
    tile_cols = columns // freq_count
    grouped = lax.all_to_all(
        smoothed.reshape(channels, strip_rows, freq_count, tile_cols),
        "freq",
        split_axis=2,
        concat_axis=0,
        tiled=True,
    )
    all_chans = channels * freq_count
    tile_data = grouped.reshape(all_chans, strip_rows * tile_cols)
    wide_tile = tile_data.astype(jnp.float32)
    total_pixels = strip_rows * columns * sky_count
    subspace = start_seed.astype(jnp.float32)
    covariance = lax.psum(local_covariance(tile_data), ("freq", "sky")) / total_pixels
    for sweep in range(ITERS):
        images = jnp.dot(covariance, subspace, precision=lax.Precision.HIGHEST)
        subspace = orthonormal(images)
    coeffs = jnp.dot(subspace.T, wide_tile, precision=lax.Precision.HIGHEST)
    cleaned = (wide_tile - jnp.dot(subspace, coeffs, precision=lax.Precision.HIGHEST)).astype(
        jnp.bfloat16
    )
    return cleaned.reshape(all_chans, 1, strip_rows * tile_cols)


def solution(mesh):
    return jax.shard_map(
        body,
        mesh=mesh,
        in_specs=(P("freq", "sky", None), P("freq"), P(), P()),
        out_specs=P(None, ("freq", "sky"), None),
        check_vma=False,
    )
```

profile of v0, /device:TPU:2, one launch (start us, length us, event | category | flops | bytes accessed | tf_op | source)
XLA Modules:
  0.0 664.6 jit_solution(16235698417459183960)
XLA Ops:
  6.5 2.9 fusion.109
  9.5 1.2 copy.36
  10.7 3.4 collective-permute-start
  14.1 1.2 copy.37
  15.2 2.6 collective-permute-start.1
  18.6 0.5 slice_reduce_fusion.30
  19.4 37.7 %collective-permute-done = bf16[16,15,4096]{2,0,1:T(8,128)(2,1)S(1)} collective-permute-done((bf16[16,15,4096]{2,0,1:T(8,128)(2,1)S(1)}, bf16[16,15,4096]{2,0,1:T(8,128)(2,1)S(1)}, u32[]{:S(2)}, u32[]{:S(2)}) %collective-permute-start) | collective-permute-done | bytes 1966112 | tf_op jit(solution)/shard_map/ppermute | solution.py:16
  57.1 1.1 copy.24
  58.2 3.2 collective-permute-done.1
  61.4 1.1 copy_dynamic-update-slice_fusion
  62.5 40.9 %multiply_add_fusion = f32[16,24,4096]{2,1,0:T(8,128)S(1)} fusion(bf16[16,24,4096]{2,1,0:T(8,128)(2,1)S(1)} %copy-done.2, bf16[16,15,4096]{2,1,0:T(8,128)(2,1)S(1)} %copy.24, bf16[16,39,4096]{2,1,0:T(8,128)(2,1)S(1)} %copy_dynamic-update-slice_fusion, f32[16]{0:T(128)S(1)} %get-tuple-element.8, f32[16]{0:T(128)S(1)} %get-tuple-element.9, ...), kind=kLoop, calls=%fused_computation.62 | loop fusion | flops 215482368 | bytes 58591168 | tf_op jit(solution)/shard_map/add | solution.py:25
  103.4 50.4 %add_convert_fusion = bf16[16,24,4096]{2,1,0:T(8,128)(2,1)S(1)} fusion(f32[16,24,4096]{2,1,0:T(8,128)S(1)} %multiply_add_fusion, f32[16]{0:T(128)S(1)} %get-tuple-element.8, f32[16]{0:T(128)S(1)} %get-tuple-element.9, f32[16]{0:T(128)S(1)} %get-tuple-element.10, f32[16]{0:T(128)S(1)} %get-tuple-element.11, f32[16]{0:T(128)S(1)} %get-tuple-element.12, ...), kind=kLoop, calls=%fused_computation.29 | loop fusion | flops 97517568 | bytes 9439168 | tf_op jit(solution)/shard_map/convert_element_type | solution.py:35
  153.8 7.9 %reshape.54 = bf16[16,24,64,64]{3,2,1,0:T(8,128)(2,1)} reshape(bf16[16,24,4096]{2,1,0:T(8,128)(2,1)S(1)} %add_convert_fusion) | data formatting | bytes 6291456 | tf_op jit(solution)/shard_map/reshape | solution.py:67
  161.7 9.5 %copy.40 = bf16[16,24,64,64]{3,1,0,2:T(8,128)(2,1)} copy(bf16[16,24,64,64]{3,2,1,0:T(8,128)(2,1)} %reshape.54) | data formatting | bytes 6291456 | tf_op jit(solution)/shard_map/reshape | solution.py:67
  171.2 9.7 %reshape.118 = bf16[64,2,12288]{2,1,0:T(2,128)(2,1)S(1)} reshape(bf16[64,16,24,64]{3,2,1,0:T(8,128)(2,1)} %bitcast.141) | data formatting | bytes 6291456
  180.9 85.0 %all_to_all.15 = bf16[64,2,12288]{2,1,0:T(2,128)(2,1)} all-to-all(bf16[64,2,12288]{2,1,0:T(2,128)(2,1)S(1)} %reshape.118), channel_id=1, replica_groups=mesh['freq'=64,'sky'=4] {'freq'}, dimensions={0} | all-to-all | bytes 6291456 | tf_op jit(solution)/shard_map/all_to_all | solution.py:66
  265.9 11.1 %reshape.119 = bf16[64,16,24,64]{3,2,1,0:T(8,128)(2,1)} reshape(bf16[64,2,12288]{2,1,0:T(2,128)(2,1)} %all_to_all.15) | data formatting | bytes 6291456
  277.0 7.4 %bitcast_bitcast_fusion = bf16[64,16,24,1,64]{4,2,1,0,3:T(8,128)(2,1)} fusion(bf16[64,16,24,64]{3,2,1,0:T(8,128)(2,1)} %reshape.119), kind=kLoop, calls=%fused_computation.224 | loop fusion | bytes 6291456 | tf_op jit(solution)/shard_map/all_to_all | solution.py:66
  284.5 7.9 %reshape.55 = bf16[1024,1536]{1,0:T(8,128)(2,1)S(1)} reshape(bf16[64,16,24,1,64]{4,2,1,0,3:T(8,128)(2,1)} %bitcast_bitcast_fusion) | data formatting | bytes 6291456 | tf_op jit(solution)/shard_map/reshape | solution.py:74
  292.4 5.4 fusion.111
  297.8 267.5 %all-reduce.3.cloned.1.call-done = f32[1024,1024]{1,0:T(8,128)} async-done(((f32[1024,1024]{1,0:T(8,128)}), f32[1024,1024]{1,0:T(8,128)}) %all-reduce.3.cloned.1.call-update) | async-done | bytes 4194320 | tf_op jit(solution)/shard_map/psum | solution.py:78
  565.3 5.9 fusion.50
  571.5 1.5 cholesky.134
  573.0 0.6 compare_reduce_fusion.7
  573.7 0.6 fusion.61
  574.3 1.2 custom-call.12
  575.8 5.9 fusion.48
  582.0 1.5 cholesky.145
  583.5 0.6 compare_reduce_fusion.6
  584.1 0.6 fusion.62
  584.8 1.2 custom-call.13
  586.3 5.9 fusion.46
  592.5 1.5 cholesky.156
  594.0 0.6 compare_reduce_fusion.5
  594.6 0.6 fusion.63
  595.3 1.2 custom-call.14
  596.8 5.9 fusion.44
  602.9 1.6 cholesky.167
  604.6 0.6 compare_reduce_fusion.4
  605.3 0.6 fusion.64
  605.9 1.2 custom-call.15
  607.4 5.9 fusion.42
  613.6 1.5 cholesky.178
  615.1 0.6 compare_reduce_fusion.3
  615.7 0.6 fusion.65
  616.4 1.2 custom-call.16
  617.9 5.9 fusion.40
  624.1 1.5 cholesky.189
  625.6 0.6 compare_reduce_fusion.2
  626.2 0.6 fusion.66
  626.9 1.2 custom-call.17
  628.4 5.9 fusion.38
  634.5 1.5 cholesky.200
  636.1 0.6 compare_reduce_fusion.1
  636.7 0.6 fusion.67
  637.4 1.2 custom-call.18
  638.9 5.9 fusion.36
  644.7 0.4 fusion.119
  645.2 1.5 cholesky.211
  646.8 0.6 compare_reduce_fusion
  647.4 0.6 fusion.68
  648.1 1.2 custom-call.19
  649.6 1.3 fusion.120
  650.9 6.7 %fusion.21 = bf16[1024,1,1536]{2,0,1:T(8,128)(2,1)} fusion(f32[1024,16]{0,1:T(8,128)S(1)} %convolution_bitcast_fusion, f32[16,1536]{1,0:T(8,128)S(1)} %fusion.120, bf16[1024,1536]{1,0:T(8,128)(2,1)S(1)} %reshape.55), kind=kOutput, calls=%fused_computation.63 | convolution fusion | flops 306708480 | bytes 6455296 | tf_op jit(solution)/shard_map/dot_general | solution.py:83
  (55 shorter events, 5.6 us)
Async XLA Ops:
  6.5 11.3 %copy-start = (f32[8,31]{1,0:T(8,128)S(1)}, f32[8,31]{1,0:T(8,128)}, u32[]{:S(2)}) copy-start(f32[8,31]{1,0:T(8,128)} %param.9) | copy-start | bytes 2980
  6.5 11.3 %copy-start.4 = (s32[16]{0:T(128)S(1)}, s32[16]{0:T(128)}, u32[]{:S(2)}) copy-start(s32[16]{0:T(128)} %param.8) | copy-start | bytes 196
  6.5 558.8 %all-reduce.3.cloned.1.call-start = ((), (), s32[]{:S(2)}) async-start(), calls=%async_computation.1 | async-start | bytes 8388608 | tf_op jit(solution)/shard_map/psum | solution.py:78
  9.5 9.6 %copy-start.2 = (bf16[16,24,4096]{2,1,0:T(8,128)(2,1)S(1)}, bf16[16,24,4096]{2,1,0:T(8,128)(2,1)}, u32[]{:S(2)}) copy-start(bf16[16,24,4096]{2,1,0:T(8,128)(2,1)} %param.7) | copy-start | bytes 9437188
  10.7 46.5 %collective-permute-start = (bf16[16,15,4096]{2,0,1:T(8,128)(2,1)S(1)}, bf16[16,15,4096]{2,0,1:T(8,128)(2,1)S(1)}, u32[]{:S(2)}, u32[]{:S(2)}) collective-permute-start(bf16[16,15,4096]{2,0,1:T(8,128)(2,1)S(1)} %copy.36), channel_id=1, source_target_pairs={{0,1},{1,2},{2,3},{4,5},{5,6},{6,7},{8,9},{9,10},{10,11},{12,13},{... | collective-permute-start | bytes 5898248 | tf_op jit(solution)/shard_map/ppermute | solution.py:16
  15.2 46.2 %collective-permute-start.1 = (bf16[16,15,4096]{2,0,1:T(8,128)(2,1)S(1)}, bf16[16,15,4096]{2,0,1:T(8,128)(2,1)S(1)}, u32[]{:S(2)}, u32[]{:S(2)}) collective-permute-start(bf16[16,15,4096]{2,0,1:T(8,128)(2,1)S(1)} %copy.37), channel_id=1, source_target_pairs={{1,0},{2,1},{3,2},{5,4},{6,5},{7,6},{9,8},{10,9},{11,10},{13,12},{... | collective-permute-start | bytes 5898248 | tf_op jit(solution)/shard_map/ppermute | solution.py:17
  292.4 273.0 %copy-start.3 = (s32[1024,16]{0,1:T(8,128)S(1)}, s32[1024,16]{0,1:T(8,128)}, u32[]{:S(2)}) copy-start(s32[1024,16]{0,1:T(8,128)} %param.10) | copy-start | bytes 196612
  638.6 18.9 %copy-start.1 = (f32[8,31]{1,0:T(8,128)S(1)}, f32[8,31]{1,0:T(8,128)}, u32[]{:S(2)}) copy-start(f32[8,31]{1,0:T(8,128)} %param.9) | copy-start | bytes 2980
Sparse Core Ops, SparseCore 0:
  297.9 267.3 all-reduce.2
where the time goes:
time: 671 us; the launch traced here: 665 us
  waiting for transfers between devices  308 us (46%)
  other arithmetic  124 us (18%)
  blocking collectives  85 us (13%)
  matrix products  64.5 us (10%)
  local copies, waits for them, and re-layouts  62.9 us (9%)
  between operations  13.9 us (2%)
    psum x1, waiting for transfers between devices, body(): lax.psum(local_covariance(tile_data), ('freq', 'sky')) / total_pixels  268 us
    all_to_all x1, blocking collectives, body(): lax.all_to_all(smoothed.reshape(channels, strip_rows, freq_count, tile_co...  85 us
    convert_element_type x1, other arithmetic, column_pass(): return col_pass.astype(jnp.bfloat16)  50.4 us
    dot_general x8, matrix products, body(): images = jnp.dot(covariance, subspace, precision=lax.Precision.HIGHEST)  47 us
    add x1, other arithmetic, column_pass(): row_pass + kernels[:, offset, None, None] * padded[:, offset:offset + str...  40.9 us
    ppermute x1, waiting for transfers between devices, with_halo(): before = lax.ppermute(last, axis, up)  37.7 us
    unnamed x15, local copies, waits for them, and re-layouts  23.5 us
    another operation x24, other arithmetic, orthonormal(): factor = jnp.linalg.cholesky(gram_matrix)  17.5 us
  transfers between devices with their start and end apart: 3, of which 3 were waited for; matrix products, arithmetic and copies ran while one was open for 1% of the time, Pallas kernels for 0%

commit v1 on v0

--- a/solution.py
+++ b/solution.py
@@ -1,9 +1,19 @@
+import functools
 import jax
 import jax.numpy as jnp
 from jax import lax
 from jax.sharding import PartitionSpec as P
 
 ITERS = 8
+
+
+def place_tokens(vals, net_axis, mesh_dim):
+    for d in (net_axis, mesh_dim):
+        vals = lax.psum(vals, d)
+    return vals
+
+
+recast_hubs = functools.partial(place_tokens, net_axis="sky", mesh_dim="freq")
 
 
 def with_halo(x, sides, width):
@@ -75,7 +85,7 @@
     wide_tile = tile_data.astype(jnp.float32)
     total_pixels = strip_rows * columns * sky_count
     subspace = start_seed.astype(jnp.float32)
-    covariance = lax.psum(local_covariance(tile_data), ("freq", "sky")) / total_pixels
+    covariance = recast_hubs(local_covariance(tile_data)) / total_pixels
     for sweep in range(ITERS):
         images = jnp.dot(covariance, subspace, precision=lax.Precision.HIGHEST)
         subspace = orthonormal(images)

time: 671 us -> 698 us (1.040)
  waiting for transfers between devices: 308 us -> 335 us
    psum x1 -> x2, waiting for transfers between devices: 268 us -> 294 us  [place_tokens(): vals = lax.psum(vals, d)]
  transfers between devices with their start and end apart: 3 -> 4, of which waited for: 3 -> 4; matrix products, arithmetic and copies ran while one was open for 1% -> 1% of each run, Pallas kernels for 0% -> 0%
where the time goes in v1:
time: 698 us; the launch traced here: 692 us
  waiting for transfers between devices  335 us (48%)
  other arithmetic  124 us (18%)
  blocking collectives  85 us (12%)
  matrix products  64.1 us (9%)
  local copies, waits for them, and re-layouts  62.9 us (9%)
  between operations  13.9 us (2%)
    psum x2, waiting for transfers between devices, place_tokens(): vals = lax.psum(vals, d)  294 us
    all_to_all x1, blocking collectives, body(): lax.all_to_all(smoothed.reshape(channels, strip_rows, freq_count, tile_co...  85 us
    convert_element_type x1, other arithmetic, column_pass(): return col_pass.astype(jnp.bfloat16)  50.4 us
    dot_general x8, matrix products, body(): images = jnp.dot(covariance, subspace, precision=lax.Precision.HIGHEST)  47.2 us
    add x1, other arithmetic, column_pass(): row_pass + kernels[:, offset, None, None] * padded[:, offset:offset + str...  40.9 us
    ppermute x1, waiting for transfers between devices, with_halo(): before = lax.ppermute(last, axis, up)  37.7 us
    unnamed x15, local copies, waits for them, and re-layouts  23.5 us
    another operation x24, other arithmetic, orthonormal(): factor = jnp.linalg.cholesky(gram_matrix)  17.5 us
  transfers between devices with their start and end apart: 4, of which 4 were waited for; matrix products, arithmetic and copies ran while one was open for 1% of the time, Pallas kernels for 0%

profile of v1, /device:TPU:2, one launch (start us, length us, event | category | flops | bytes accessed | tf_op | source)
XLA Modules:
  0.0 691.6 jit_solution(10457013735751264317)
XLA Ops:
  6.5 2.9 fusion.109
  9.5 1.2 copy.36
  10.7 3.4 collective-permute-start
  14.1 1.2 copy.37
  15.2 2.6 collective-permute-start.1
  18.6 0.5 slice_reduce_fusion.30
  19.4 37.7 %collective-permute-done = bf16[16,15,4096]{2,0,1:T(8,128)(2,1)S(1)} collective-permute-done((bf16[16,15,4096]{2,0,1:T(8,128)(2,1)S(1)}, bf16[16,15,4096]{2,0,1:T(8,128)(2,1)S(1)}, u32[]{:S(2)}, u32[]{:S(2)}) %collective-permute-start) | collective-permute-done | bytes 1966112 | tf_op jit(solution)/shard_map/ppermute | solution.py:26
  57.1 1.1 copy.24
  58.2 3.2 collective-permute-done.1
  61.4 1.1 copy_dynamic-update-slice_fusion
  62.5 40.9 %multiply_add_fusion = f32[16,24,4096]{2,1,0:T(8,128)S(1)} fusion(bf16[16,24,4096]{2,1,0:T(8,128)(2,1)S(1)} %copy-done.2, bf16[16,15,4096]{2,1,0:T(8,128)(2,1)S(1)} %copy.24, bf16[16,39,4096]{2,1,0:T(8,128)(2,1)S(1)} %copy_dynamic-update-slice_fusion, f32[16]{0:T(128)S(1)} %get-tuple-element.8, f32[16]{0:T(128)S(1)} %get-tuple-element.9, ...), kind=kLoop, calls=%fused_computation.62 | loop fusion | flops 215482368 | bytes 58591168 | tf_op jit(solution)/shard_map/add | solution.py:35
  103.4 50.4 %add_convert_fusion = bf16[16,24,4096]{2,1,0:T(8,128)(2,1)S(1)} fusion(f32[16,24,4096]{2,1,0:T(8,128)S(1)} %multiply_add_fusion, f32[16]{0:T(128)S(1)} %get-tuple-element.8, f32[16]{0:T(128)S(1)} %get-tuple-element.9, f32[16]{0:T(128)S(1)} %get-tuple-element.10, f32[16]{0:T(128)S(1)} %get-tuple-element.11, f32[16]{0:T(128)S(1)} %get-tuple-element.12, ...), kind=kLoop, calls=%fused_computation.29 | loop fusion | flops 97517568 | bytes 9439168 | tf_op jit(solution)/shard_map/convert_element_type | solution.py:45
  153.8 7.9 %reshape.54 = bf16[16,24,64,64]{3,2,1,0:T(8,128)(2,1)} reshape(bf16[16,24,4096]{2,1,0:T(8,128)(2,1)S(1)} %add_convert_fusion) | data formatting | bytes 6291456 | tf_op jit(solution)/shard_map/reshape | solution.py:77
  161.7 9.5 %copy.40 = bf16[16,24,64,64]{3,1,0,2:T(8,128)(2,1)} copy(bf16[16,24,64,64]{3,2,1,0:T(8,128)(2,1)} %reshape.54) | data formatting | bytes 6291456 | tf_op jit(solution)/shard_map/reshape | solution.py:77
  171.2 9.7 %reshape.118 = bf16[64,2,12288]{2,1,0:T(2,128)(2,1)S(1)} reshape(bf16[64,16,24,64]{3,2,1,0:T(8,128)(2,1)} %bitcast.141) | data formatting | bytes 6291456
  180.9 85.0 %all_to_all.15 = bf16[64,2,12288]{2,1,0:T(2,128)(2,1)} all-to-all(bf16[64,2,12288]{2,1,0:T(2,128)(2,1)S(1)} %reshape.118), channel_id=1, replica_groups=mesh['freq'=64,'sky'=4] {'freq'}, dimensions={0} | all-to-all | bytes 6291456 | tf_op jit(solution)/shard_map/all_to_all | solution.py:76
  265.9 11.1 %reshape.119 = bf16[64,16,24,64]{3,2,1,0:T(8,128)(2,1)} reshape(bf16[64,2,12288]{2,1,0:T(2,128)(2,1)} %all_to_all.15) | data formatting | bytes 6291456
  277.0 7.4 %bitcast_bitcast_fusion = bf16[64,16,24,1,64]{4,2,1,0,3:T(8,128)(2,1)} fusion(bf16[64,16,24,64]{3,2,1,0:T(8,128)(2,1)} %reshape.119), kind=kLoop, calls=%fused_computation.224 | loop fusion | bytes 6291456 | tf_op jit(solution)/shard_map/all_to_all | solution.py:76
  284.5 7.9 %reshape.55 = bf16[1024,1536]{1,0:T(8,128)(2,1)S(1)} reshape(bf16[64,16,24,1,64]{4,2,1,0,3:T(8,128)(2,1)} %bitcast_bitcast_fusion) | data formatting | bytes 6291456 | tf_op jit(solution)/shard_map/reshape | solution.py:84
  292.4 5.0 fusion.111
  297.9 93.7 %all-reduce.4.cloned.1.call-done = f32[1024,1024]{1,0:T(8,128)} async-done(((f32[1024,1024]{1,0:T(8,128)}), f32[1024,1024]{1,0:T(8,128)}) %all-reduce.4.cloned.1.call-update) | async-done | bytes 4194320 | tf_op jit(solution)/shard_map/psum | solution.py:12
  391.6 200.7 %all-reduce.6.cloned.1.call-done = f32[1024,1024]{1,0:T(8,128)} async-done(((f32[1024,1024]{1,0:T(8,128)}), f32[1024,1024]{1,0:T(8,128)}) %all-reduce.6.cloned.1.call-update) | async-done | bytes 4194320 | tf_op jit(solution)/shard_map/psum | solution.py:12
  592.4 5.9 fusion.50
  598.5 1.5 cholesky.134
  600.0 0.6 compare_reduce_fusion.7
  600.7 0.6 fusion.61
  601.3 1.2 custom-call.12
  602.8 5.9 fusion.48
  609.0 1.5 cholesky.145
  610.5 0.6 compare_reduce_fusion.6
  611.2 0.6 fusion.62
  611.8 1.2 custom-call.13
  613.3 5.9 fusion.46
  619.5 1.5 cholesky.156
  621.0 0.6 compare_reduce_fusion.5
  621.6 0.6 fusion.63
  622.3 1.2 custom-call.14
  623.8 5.9 fusion.44
  630.0 1.6 cholesky.167
  631.6 0.6 compare_reduce_fusion.4
  632.3 0.6 fusion.64
  632.9 1.2 custom-call.15
  634.4 5.9 fusion.42
  640.6 1.5 cholesky.178
  642.1 0.6 compare_reduce_fusion.3
  642.8 0.6 fusion.65
  643.4 1.2 custom-call.16
  644.9 5.9 fusion.40
  651.1 1.5 cholesky.189
  652.6 0.6 compare_reduce_fusion.2
  653.2 0.6 fusion.66
  653.9 1.2 custom-call.17
  655.4 5.9 fusion.38
  661.6 1.5 cholesky.200
  663.1 0.6 compare_reduce_fusion.1
  663.7 0.6 fusion.67
  664.4 1.2 custom-call.18
  665.9 6.1 fusion.36
  672.2 1.5 cholesky.211
  673.8 0.6 compare_reduce_fusion
  674.4 0.6 fusion.68
  675.1 1.2 custom-call.19
  676.6 1.3 fusion.120
  677.9 6.7 fusion.21
  (58 shorter events, 6.2 us)
Async XLA Ops:
  6.5 11.3 %copy-start = (f32[8,31]{1,0:T(8,128)S(1)}, f32[8,31]{1,0:T(8,128)}, u32[]{:S(2)}) copy-start(f32[8,31]{1,0:T(8,128)} %param.9) | copy-start | bytes 2980
  6.5 11.3 %copy-start.4 = (s32[16]{0:T(128)S(1)}, s32[16]{0:T(128)}, u32[]{:S(2)}) copy-start(s32[16]{0:T(128)} %param.8) | copy-start | bytes 196
  6.5 385.1 %all-reduce.4.cloned.1.call-start = ((), (), s32[]{:S(2)}) async-start(), calls=%async_computation.1 | async-start | bytes 8388608 | tf_op jit(solution)/shard_map/psum | solution.py:12
  9.5 9.6 %copy-start.2 = (bf16[16,24,4096]{2,1,0:T(8,128)(2,1)S(1)}, bf16[16,24,4096]{2,1,0:T(8,128)(2,1)}, u32[]{:S(2)}) copy-start(bf16[16,24,4096]{2,1,0:T(8,128)(2,1)} %param.7) | copy-start | bytes 9437188
  10.7 46.5 %collective-permute-start = (bf16[16,15,4096]{2,0,1:T(8,128)(2,1)S(1)}, bf16[16,15,4096]{2,0,1:T(8,128)(2,1)S(1)}, u32[]{:S(2)}, u32[]{:S(2)}) collective-permute-start(bf16[16,15,4096]{2,0,1:T(8,128)(2,1)S(1)} %copy.36), channel_id=1, source_target_pairs={{0,1},{1,2},{2,3},{4,5},{5,6},{6,7},{8,9},{9,10},{10,11},{12,13},{... | collective-permute-start | bytes 5898248 | tf_op jit(solution)/shard_map/ppermute | solution.py:26
  15.2 46.2 %collective-permute-start.1 = (bf16[16,15,4096]{2,0,1:T(8,128)(2,1)S(1)}, bf16[16,15,4096]{2,0,1:T(8,128)(2,1)S(1)}, u32[]{:S(2)}, u32[]{:S(2)}) collective-permute-start(bf16[16,15,4096]{2,0,1:T(8,128)(2,1)S(1)} %copy.37), channel_id=1, source_target_pairs={{1,0},{2,1},{3,2},{5,4},{6,5},{7,6},{9,8},{10,9},{11,10},{13,12},{... | collective-permute-start | bytes 5898248 | tf_op jit(solution)/shard_map/ppermute | solution.py:27
  297.4 294.9 %copy-start.3 = (s32[1024,16]{0,1:T(8,128)S(1)}, s32[1024,16]{0,1:T(8,128)}, u32[]{:S(2)}) copy-start(s32[1024,16]{0,1:T(8,128)} %param.10) | copy-start | bytes 196612
  297.5 294.9 %all-reduce.6.cloned.1.call-start = ((), (), s32[]{:S(2)}) async-start(), calls=%async_computation.2 | async-start | bytes 8388608 | tf_op jit(solution)/shard_map/psum | solution.py:12
  665.6 18.9 %copy-start.1 = (f32[8,31]{1,0:T(8,128)S(1)}, f32[8,31]{1,0:T(8,128)}, u32[]{:S(2)}) copy-start(f32[8,31]{1,0:T(8,128)} %param.9) | copy-start | bytes 2980
Sparse Core Ops, SparseCore 0:
  297.6 93.9 all-reduce.3
  395.1 197.1 all-reduce.5
